TPU v7x, 256 devices: a whole 4x4x8 slice. The times are simulated.
256 devices in a mesh: seg: 8 (over z_hi, core), shard: 16 (over x, y), tok: 2 (over z_lo).
Axes of the slice: x: 4, y: 4, z: 8 (z_hi: 4, z_lo: 2; z = z_hi * 2 + z_lo), core: 2. Of those that a mesh axis runs over, the one named last changes fastest.
Arguments:
- activations: bfloat16 [768, 2560], P('tok', 'shard'), may hold values from -6 to 6
- gate_weight: bfloat16 [2560, 10240], P('shard', 'seg'), may hold values from -0.125 to 0.125
- up_weight: bfloat16 [2560, 10240], P('shard', 'seg'), may hold values from -0.125 to 0.125
- down_weight: bfloat16 [10240, 2560], P('seg', 'shard'), may hold values from -0.0625 to 0.0625
- encoder_weight: bfloat16 [2560, 65536], P(None, ('seg', 'shard')), may hold values from -0.125 to 0.125
- encoder_bias: float32 [65536], P(('seg', 'shard')), may hold values from -0.6 to 0.2
- decoder_weight: bfloat16 [65536, 2560], P(('seg', 'shard')), may hold values from -0.0625 to 0.0625
- decoder_bias: float32 [2560], replicated, may hold values from -1.5 to 1.5
- segment_sizes: int32 [8], replicated, may hold values from 4096 to 8192, as said below
Outputs:
- grad_encoder: float32 [2560, 65536], P('tok', ('seg', 'shard'))
- grad_decoder: float32 [65536, 2560], P(('seg', 'shard'), 'tok')
- prefix_mse: float32 [8], P('seg')
Inputs may be any that keep to these rules, and one draw needn't show every extreme that they name: `segment_sizes`: at least one segment has all 8192 latents live.
All inputs are finite; a program needn't handle non-finite values.
Results may differ from a plain program's by a relative error of at most 0.0078.
Values may be sent and summed in bfloat16 or wider, within the bound.
No kernel may reach another device: no remote copies, remote signals or barrier semaphores. Data moves between devices by JAX's collectives and lax.ppermute only.
A program may use at most 64 MiB of HBM per device.

v0:
```python
import math
import jax
import jax.numpy as jnp
from jax import lax
from jax.sharding import PartitionSpec as P


def carried_in(value, axis, join, neutral, backward):
    count, mine = (lax.axis_size(axis), lax.axis_index(axis))
    pieces = lax.all_gather(value, axis)
    if backward:
        pieces = pieces[::-1]
        mine = count - 1 - mine
    subtotal = jnp.full_like(value, 0) + jnp.asarray(neutral, value.dtype)

    def hop(position, subtotal):
        longer = join(subtotal, pieces[position])
        return jnp.where(position < mine, longer, subtotal)

    return lax.fori_loop(0, count - 1, hop, subtotal)


def local(
    activations,
    gate_weight,
    up_weight,
    down_weight,
    encoder_weight,
    encoder_bias,
    decoder_weight,
    decoder_bias,
    segment_sizes,
):
    shard_index = lax.axis_index("shard")
    segment_index = lax.axis_index("seg")
    tok_rows = activations.shape[0]
    width_slice = activations.shape[1]
    gate_part = jnp.dot(activations, gate_weight, preferred_element_type=jnp.float32)
    up_part = jnp.dot(activations, up_weight, preferred_element_type=jnp.float32)
    gate_total, up_total = lax.psum((gate_part, up_part), "shard")
    hidden = (jax.nn.gelu(gate_total, approximate=True) * up_total).astype(jnp.bfloat16)
    down_part = jnp.dot(hidden, down_weight, preferred_element_type=jnp.float32)
    mlp_slice = lax.psum(down_part, "seg").astype(jnp.bfloat16)
    mlp_full = lax.all_gather(mlp_slice, "shard", axis=1, tiled=True)
    width = mlp_full.shape[1]
    groups = lax.axis_size("tok")
    tokens_all = tok_rows * groups
    mlp_float = mlp_full.astype(jnp.float32)
    centered = (mlp_float - decoder_bias).astype(jnp.bfloat16)
    lat_count = encoder_weight.shape[1]
    segment_total = segment_sizes.shape[0]
    size_here = jnp.sum(jnp.where(jnp.arange(segment_total) == segment_index, segment_sizes, 0))
    latent_index = shard_index * lat_count + jnp.arange(lat_count)
    live_mask = latent_index < size_here
    pre_act = jnp.dot(centered, encoder_weight, preferred_element_type=jnp.float32) + encoder_bias
    latent_codes = jnp.where(live_mask, jax.nn.softplus(10.0 * pre_act) / 10.0, 0.0).astype(
        jnp.bfloat16
    )
    slope = jnp.where(live_mask, jax.nn.sigmoid(10.0 * pre_act), 0.0)
    columns = decoder_weight
    my_part = lax.psum_scatter(
        lax.dot_general(
            columns, latent_codes, (((0,), (1,)), ((), ())), preferred_element_type=jnp.float32
        ),
        "shard",
        scatter_dimension=0,
        tiled=True,
    )
    column_start = shard_index * width_slice
    target = lax.dynamic_slice_in_dim(mlp_float, column_start, width_slice, 1).T
    bias_slice = lax.dynamic_slice_in_dim(decoder_bias, column_start, width_slice, 0)[:, None]
    blank = jnp.zeros_like(my_part)
    earlier = carried_in(my_part, "seg", jnp.add, blank, False)
    errors = bias_slice + (earlier + my_part) - target
    total_square = lax.psum(jnp.sum(errors * errors), ("shard", "tok"))
    prefix_mse = (total_square / (tokens_all * width)).reshape(1)
    later = carried_in(errors, "seg", jnp.add, blank, True)
    back = ((later + errors) * (1.0 / math.sqrt(tokens_all))).astype(jnp.bfloat16)
    piece = lax.all_gather(back, "shard", axis=0, tiled=True)
    columns = decoder_weight
    code_acc = lax.dot_general(
        piece, columns, (((0,), (1,)), ((), ())), preferred_element_type=jnp.float32
    )
    grad_piece = lax.dot_general(
        latent_codes, piece, (((0,), (1,)), ((), ())), preferred_element_type=jnp.float32
    )
    code_grad = (code_acc * slope).astype(jnp.bfloat16)
    encoder_grad = lax.dot_general(
        centered, code_grad, (((0,), (0,)), ((), ())), preferred_element_type=jnp.float32
    )
    grad_encoder = lax.psum_scatter(encoder_grad, "tok", scatter_dimension=0, tiled=True)
    grad_decoder = lax.psum_scatter(grad_piece, "tok", scatter_dimension=1, tiled=True)
    return (grad_encoder, grad_decoder, prefix_mse)


def solution(mesh):
    in_specs = (
        P("tok", "shard"),
        P("shard", "seg"),
        P("shard", "seg"),
        P("seg", "shard"),
        P(None, ("seg", "shard")),
        P(("seg", "shard")),
        P(("seg", "shard"), None),
        P(),
        P(),
    )
    out_specs = (P("tok", ("seg", "shard")), P(("seg", "shard"), "tok"), P("seg"))
    return jax.shard_map(local, mesh=mesh, in_specs=in_specs, out_specs=out_specs, check_vma=False)
```

profile of v0, /device:TPU:1, one launch (start us, length us, event | category | flops | bytes accessed | tf_op | source)
XLA Modules:
  0.0 602.7 jit_solution(8608097557932764812)
XLA Ops:
  7.2 2.9 fusion.35
  10.2 1.7 fusion.36
  12.0 0.0 all-gather.7.cloned.1.call-start
  12.0 114.8 %all-reduce.4.cloned.1.call-done = (f32[384,1280]{1,0:T(8,128)}, f32[384,1280]{1,0:T(8,128)}) async-done(((f32[384,1280]{1,0:T(8,128)}, f32[384,1280]{1,0:T(8,128)}), (f32[384,1280]{1,0:T(8,128)}, f32[384,1280]{1,0:T(8,128)})) %all-reduce.4.cloned.1.call-update) | async-done | bytes 3932176 | tf_op jit(solution)/shard_map/psum | solution.py:40
  126.8 3.1 fusion.12
  129.8 30.9 %all-reduce.5 = bf16[384,160]{0,1:T(8,128)(2,1)} all-reduce(f32[384,160]{0,1:T(8,128)S(1)} %fusion.12), channel_id=1, replica_groups=mesh['seg'=8,'shard'=16,'tok'=2] {'seg'}, use_global_device_ids=true, to_apply=%region_2.0 | all-reduce | flops 61440 | bytes 368640 | tf_op jit(solution)/shard_map/psum | solution.py:43
  160.7 0.0 reduce-scatter.4.cloned.1.call-start
  160.8 0.6 fusion.25
  161.4 0.7 add_compare_fusion
  162.1 47.5 %all-gather.7.cloned.1.call-done = bf16[384,2560]{0,1:T(8,128)(2,1)} async-done(((bf16[384,160]{0,1:T(8,128)(2,1)}), bf16[384,2560]{0,1:T(8,128)(2,1)}) %all-gather.7.cloned.1.call-update) | async-done | bytes 1966096 | tf_op jit(solution)/shard_map/all_gather | solution.py:44
  209.6 4.0 fusion.9
  213.6 0.9 copy-done.1
  214.5 3.6 convolution_bitcast_fusion
  218.2 0.0 all-gather.11.cloned.1.call-start
  218.2 82.0 %reduce-scatter.4.cloned.1.call-done = f32[160,384]{1,0:T(8,128)} async-done(((f32[2560,384]{1,0:T(8,128)}), f32[160,384]{1,0:T(8,128)}) %reduce-scatter.4.cloned.1.call-update) | async-done | bytes 245776 | tf_op jit(solution)/shard_map/reduce_scatter | solution.py:61
  300.2 0.0 all-gather.13.cloned.1.call-start
  300.3 0.1 dynamic_slice.20
  300.3 3.7 convert_element_type.23
  304.0 33.6 %all-gather.11.cloned.1.call-done = f32[1280,384]{1,0:T(8,128)} async-done(((f32[160,384]{1,0:T(8,128)}), f32[1280,384]{1,0:T(8,128)}) %all-gather.11.cloned.1.call-update) | async-done | bytes 1966096 | tf_op jit(solution)/shard_map/all_gather | solution.py:10
  337.6 7.2 %while.28 = (s32[]{:T(128)}, f32[160,384]{1,0:T(8,128)S(1)}, s32[]{:T(128)}, f32[8,160,384]{2,1,0:T(8,128)}, s32[]{:T(128)}, /*index=5*/s32[]{:T(128)}) while((s32[]{:T(128)}, f32[160,384]{1,0:T(8,128)S(1)}, s32[]{:T(128)}, f32[8,160,384]{2,1,0:T(8,128)}, s32[]{:T(128)}, /*index=5*/s32[]{:T(128)}) %tuple.87), condition=%wide.region_6.7_spmd.clone, body=%wide.region_5.6_spmd.clone.sunk | while | flops 184324 | bytes 737381 | solution.py:20
  337.6 1.0 add_select_fusion.4
  338.7 1.0 add_select_fusion.4
  339.7 1.0 add_select_fusion.4
  340.7 1.0 add_select_fusion.4
  341.8 1.0 add_select_fusion.4
  342.8 1.0 add_select_fusion.4
  343.9 1.0 add_select_fusion.4
  344.9 2.3 multiply_reduce_fusion
  347.2 0.0 all-gather.9.cloned.1.call-start
  347.3 33.5 %all-gather.13.cloned.1.call-done = f32[1280,384]{1,0:T(8,128)} async-done(((f32[160,384]{1,0:T(8,128)}), f32[1280,384]{1,0:T(8,128)}) %all-gather.13.cloned.1.call-update) | async-done | bytes 1966096 | tf_op jit(solution)/shard_map/all_gather | solution.py:10
  380.7 3.0 rev.3
  383.7 7.3 %while.29 = (s32[]{:T(128)}, f32[160,384]{1,0:T(8,128)S(1)}, s32[]{:T(128)}, f32[8,160,384]{2,1,0:T(8,128)}, s32[]{:T(128)}, /*index=5*/s32[]{:T(128)}) while((s32[]{:T(128)}, f32[160,384]{1,0:T(8,128)S(1)}, s32[]{:T(128)}, f32[8,160,384]{2,1,0:T(8,128)}, s32[]{:T(128)}, /*index=5*/s32[]{:T(128)}) %tuple.67), condition=%wide.region_8.9_spmd.clone, body=%wide.region_7.8_spmd.clone.sunk | while | flops 184324 | bytes 737381 | solution.py:20
  383.7 1.1 add_select_fusion.5
  384.8 1.0 add_select_fusion.5
  385.8 1.0 add_select_fusion.5
  386.8 1.0 add_select_fusion.5
  387.9 1.0 add_select_fusion.5
  388.9 1.0 add_select_fusion.5
  390.0 1.0 add_select_fusion.5
  391.0 0.7 multiply_convert_fusion
  391.7 0.0 reduce-scatter.6.cloned.1.call-start
  391.8 47.0 %all-gather.9.cloned.1.call-done = bf16[2560,384]{1,0:T(8,128)(2,1)} async-done(((bf16[160,384]{1,0:T(8,128)(2,1)}), bf16[2560,384]{1,0:T(8,128)(2,1)}) %all-gather.9.cloned.1.call-update) | async-done | bytes 1966096 | tf_op jit(solution)/shard_map/all_gather | solution.py:79
  438.7 7.3 %fusion.11 = f32[2560,512]{1,0:T(8,128)} fusion(bf16[2560,384]{1,0:T(8,128)(2,1)} %all-gather.9.cloned.1.call-done, bf16[512,2560]{1,0:T(8,128)(2,1)S(1)} %copy-done, f32[2560]{0:T(1024)S(1)} %copy-done.7, bf16[384,2560]{0,1:T(8,128)(2,1)} %all-gather.7.cloned.1.call-done, f32[384,512]{1,0:T(8,128)} %copy-done.1, pred[512]{0:T(512)(128)(4,1)S(1)} %add_compare_fusion), kind=kOutput, calls=%fused_computation.19 | convolution fusion | flops 2017394688 | bytes 12593664 | tf_op jit(solution)/shard_map/dot_general | solution.py:88
  446.1 0.0 reduce-scatter.8.cloned.1.call-start
  446.1 1.1 copy-done.2
  447.2 5.7 fusion.32
  453.0 71.1 %psum.31 = f32[]{:T(128)} all-reduce(f32[]{:T(128)} %get-tuple-element.211), channel_id=1, replica_groups=mesh['seg'=8,'shard'=16,'tok'=2] {'shard','tok'}, use_global_device_ids=true, to_apply=%region_12.13 | all-reduce | flops 1 | bytes 8 | tf_op jit(solution)/shard_map/psum | solution.py:75
  524.8 69.9 %reduce-scatter.8.cloned.1.call-done = f32[512,1280]{1,0:T(8,128)} async-done(((f32[512,2560]{1,0:T(8,128)}), f32[512,1280]{1,0:T(8,128)}) %reduce-scatter.8.cloned.1.call-update) | async-done | bytes 2621456 | tf_op jit(solution)/shard_map/reduce_scatter | solution.py:92
  (32 shorter events, 0.2 us)
Async XLA Ops:
  7.2 207.4 %copy-start = (bf16[512,2560]{1,0:T(8,128)(2,1)S(1)}, bf16[512,2560]{1,0:T(8,128)(2,1)}, u32[]{:S(2)}) copy-start(bf16[512,2560]{1,0:T(8,128)(2,1)} %param.19) | copy-start | bytes 7864324
  7.2 3.0 copy-start.5
  7.2 3.0 copy-start.6
  7.2 119.6 %all-reduce.4.cloned.1.call-start = ((), (), s32[]{:S(2)}) async-start(), calls=%async_computation.10 | async-start | bytes 7864320 | tf_op jit(solution)/shard_map/psum | solution.py:40
  11.9 114.8 %copy-start.8 = (bf16[1280,160]{0,1:T(8,128)(2,1)S(1)}, bf16[1280,160]{0,1:T(8,128)(2,1)}, u32[]{:S(2)}) copy-start(bf16[1280,160]{0,1:T(8,128)(2,1)} %param.16) | copy-start | bytes 1228804
  12.0 197.6 %all-gather.7.cloned.1.call-start = ((), (), s32[]{:S(2)}) async-start(), calls=%async_computation.3 | async-start | bytes 2088960 | tf_op jit(solution)/shard_map/all_gather | solution.py:44
  126.8 34.0 %copy-start.10 = (s32[8]{0:T(128)S(1)}, s32[8]{0:T(128)}, u32[]{:S(2)}) copy-start(s32[8]{0:T(128)} %param.21) | copy-start | bytes 100
  126.8 82.8 %copy-start.7 = (f32[2560]{0:T(1024)S(1)}, f32[2560]{0:T(1024)}, u32[]{:S(2)}) copy-start(f32[2560]{0:T(1024)} %param.20) | copy-start | bytes 30724
  126.8 82.8 %copy-start.9 = (f32[512]{0:T(512)S(1)}, f32[512]{0:T(512)}, u32[]{:S(2)}) copy-start(f32[512]{0:T(512)} %param.18) | copy-start | bytes 6148
  160.7 139.5 %reduce-scatter.4.cloned.1.call-start = ((), (), s32[]{:S(2)}) async-start(), calls=%async_computation.4 | async-start | bytes 4177920 | tf_op jit(solution)/shard_map/reduce_scatter | solution.py:61
  213.6 0.9 copy-start.1
  218.2 119.5 %all-gather.11.cloned.1.call-start = ((), (), s32[]{:S(2)}) async-start(), calls=%async_computation.8 | async-start | bytes 2211840 | tf_op jit(solution)/shard_map/all_gather | solution.py:10
  300.2 80.5 %all-gather.13.cloned.1.call-start = ((), (), s32[]{:S(2)}) async-start(), calls=%async_computation.9 | async-start | bytes 2211840 | tf_op jit(solution)/shard_map/all_gather | solution.py:10
  304.0 40.9 %copy-start.4 = (f32[160,384]{1,0:T(8,128)S(1)}, f32[160,384]{1,0:T(8,128)}, u32[]{:S(2)}) copy-start(f32[160,384]{1,0:T(8,128)} %reduce-scatter.4.cloned.1.call-done) | copy-start | bytes 737284
  347.2 91.5 %all-gather.9.cloned.1.call-start = ((), (), s32[]{:S(2)}) async-start(), calls=%async_computation.5 | async-start | bytes 2088960 | tf_op jit(solution)/shard_map/all_gather | solution.py:79
  383.7 7.3 %copy-start.3 = (f32[160,384]{1,0:T(8,128)S(1)}, f32[160,384]{1,0:T(8,128)}, u32[]{:S(2)}) copy-start(f32[160,384]{1,0:T(8,128)} %get-tuple-element.212) | copy-start | bytes 737284
  391.7 133.0 %reduce-scatter.6.cloned.1.call-start = ((), (), s32[]{:S(2)}) async-start(), calls=%async_computation.6 | async-start | bytes 7864320 | tf_op jit(solution)/shard_map/reduce_scatter | solution.py:91
  446.1 1.1 copy-start.2
  446.1 148.6 %reduce-scatter.8.cloned.1.call-start = ((), (), s32[]{:S(2)}) async-start(), calls=%async_computation.7 | async-start | bytes 7864320 | tf_op jit(solution)/shard_map/reduce_scatter | solution.py:92
Sparse Core Ops, SparseCore 0:
  12.1 114.6 all-reduce.3
  160.8 48.6 all-gather.6
  218.3 81.8 reduce-scatter.3
  301.9 35.7 all-gather.10
  347.3 33.3 all-gather.12
  391.8 46.8 all-gather.8
  446.2 73.8 reduce-scatter.5
  523.2 71.4 reduce-scatter.7
where the time goes:
time: 603 us
  waiting for transfers between devices  428 us (71%)
  blocking collectives  102 us (17%)
  matrix products  28.5 us (5%)
  other arithmetic  22.2 us (4%)
  between operations  16.1 us (3%)
    psum x1, waiting for transfers between devices, local(): gate_total, up_total = lax.psum((gate_part, up_part), 'shard')  115 us
    reduce_scatter x1, waiting for transfers between devices, local(): lax.psum_scatter(lax.dot_general(columns, latent_codes, (((0,), (1,)), ((...  82 us
    psum x1, blocking collectives, local(): total_square = lax.psum(jnp.sum(errors * errors), ('shard', 'tok'))  71.1 us
    reduce_scatter x1, waiting for transfers between devices, local(): lax.psum_scatter(grad_piece, 'tok', scatter_dimension=1, tiled=True)  69.9 us
    all_gather x2, waiting for transfers between devices, carried_in(): pieces = lax.all_gather(value, axis)  67.1 us
    all_gather x1, waiting for transfers between devices, local(): mlp_full = lax.all_gather(mlp_slice, 'shard', axis=1, tiled=True)  47.5 us
    all_gather x1, waiting for transfers between devices, local(): piece = lax.all_gather(back, 'shard', axis=0, tiled=True)  47 us
    psum x1, blocking collectives, local(): mlp_slice = lax.psum(down_part, 'seg').astype(jnp.bfloat16)  30.9 us
  transfers between devices with their start and end apart: 8, of which 7 were waited for; matrix products, arithmetic and copies ran while one was open for 2% of the time, Pallas kernels for 0%

commit v1 on v0

--- a/solution.py
+++ b/solution.py
@@ -3,6 +3,7 @@
 import jax.numpy as jnp
 from jax import lax
 from jax.sharding import PartitionSpec as P
+from jax.lax import all_to_all, axis_size
 
 
 def carried_in(value, axis, join, neutral, backward):
@@ -41,7 +42,15 @@
     hidden = (jax.nn.gelu(gate_total, approximate=True) * up_total).astype(jnp.bfloat16)
     down_part = jnp.dot(hidden, down_weight, preferred_element_type=jnp.float32)
     mlp_slice = lax.psum(down_part, "seg").astype(jnp.bfloat16)
-    mlp_full = lax.all_gather(mlp_slice, "shard", axis=1, tiled=True)
+    mlp_full = jnp.concatenate(
+        all_to_all(
+            jnp.stack([mlp_slice] * axis_size("shard")),
+            axis_name="shard",
+            split_axis=0,
+            concat_axis=0,
+        ),
+        axis=1,
+    )
     width = mlp_full.shape[1]
     groups = lax.axis_size("tok")
     tokens_all = tok_rows * groups

time: 603 us -> 591 us (0.980)
  waiting for transfers between devices: 428 us -> 405 us
  local copies, waits for them, and re-layouts: 5.01 us -> 12.3 us
    reduce_scatter x1, waiting for transfers between devices: 69.9 us -> 0.02 us  [local(): lax.psum_scatter(grad_piece, 'tok', scatter_dimension=1, tiled=True)]
    reduce_scatter x1, waiting for transfers between devices: 0.02 us -> 69.1 us  [local(): lax.psum_scatter(encoder_grad, 'tok', scatter_dimension=0, tiled=True)]
    all_gather x1 -> x0, waiting for transfers between devices: 47.5 us -> none  [local(): mlp_full = lax.all_gather(mlp_slice, 'shard', axis=1, tiled=True)]
    all_to_all x0 -> x1, waiting for transfers between devices: none -> 20.8 us  [local(): all_to_all(jnp.stack([mlp_slice] * axis_size('shard')), axis_name='shard'...]
where the time goes in v1:
time: 591 us; the launch traced here: 590 us
  waiting for transfers between devices  405 us (69%)
  blocking collectives  101 us (17%)
  matrix products  25.4 us (4%)
  other arithmetic  24.5 us (4%)
  between operations  16.1 us (3%)
  local copies, waits for them, and re-layouts  12.3 us (2%)
    psum x1, waiting for transfers between devices, local(): gate_total, up_total = lax.psum((gate_part, up_part), 'shard')  115 us
    reduce_scatter x1, waiting for transfers between devices, local(): lax.psum_scatter(lax.dot_general(columns, latent_codes, (((0,), (1,)), ((...  86.4 us
    psum x1, blocking collectives, local(): total_square = lax.psum(jnp.sum(errors * errors), ('shard', 'tok'))  70.6 us
    reduce_scatter x1, waiting for transfers between devices, local(): lax.psum_scatter(encoder_grad, 'tok', scatter_dimension=0, tiled=True)  69.1 us
    all_gather x2, waiting for transfers between devices, carried_in(): pieces = lax.all_gather(value, axis)  67.1 us
    all_gather x1, waiting for transfers between devices, local(): piece = lax.all_gather(back, 'shard', axis=0, tiled=True)  47 us
    psum x1, blocking collectives, local(): mlp_slice = lax.psum(down_part, 'seg').astype(jnp.bfloat16)  30.3 us
    all_to_all x1, waiting for transfers between devices, local(): all_to_all(jnp.stack([mlp_slice] * axis_size('shard')), axis_name='shard'...  20.8 us
  transfers between devices with their start and end apart: 8, of which 7 were waited for; matrix products, arithmetic and copies ran while one was open for 2% of the time, Pallas kernels for 0%

profile of v1, /device:TPU:1, one launch (start us, length us, event | category | flops | bytes accessed | tf_op | source)
XLA Modules:
  0.0 590.3 jit_solution(4445514155783429900)
XLA Ops:
  7.2 2.9 fusion.35
  10.2 1.7 fusion.36
  12.0 114.8 %all-reduce.4.cloned.1.call-done = (f32[384,1280]{1,0:T(8,128)}, f32[384,1280]{1,0:T(8,128)}) async-done(((f32[384,1280]{1,0:T(8,128)}, f32[384,1280]{1,0:T(8,128)}), (f32[384,1280]{1,0:T(8,128)}, f32[384,1280]{1,0:T(8,128)})) %all-reduce.4.cloned.1.call-update) | async-done | bytes 3932176 | tf_op jit(solution)/shard_map/psum | solution.py:41
  126.8 3.0 fusion.12
  129.8 30.3 %all-reduce.5 = bf16[384,160]{0,1:T(8,128)(2,1)S(1)} all-reduce(f32[384,160]{0,1:T(8,128)S(1)} %fusion.12), channel_id=1, replica_groups=mesh['seg'=8,'shard'=16,'tok'=2] {'seg'}, use_global_device_ids=true, to_apply=%region_2.0 | all-reduce | flops 61440 | bytes 368640 | tf_op jit(solution)/shard_map/psum | solution.py:44
  160.1 1.4 stack.2
  161.6 5.3 all-to-all-start
  166.9 0.6 fusion.25
  167.6 0.7 add_compare_fusion
  168.2 20.8 %all-to-all-done = bf16[16,384,160]{1,2,0:T(8,128)(2,1)} async-done(((bf16[16,384,160]{1,2,0:T(8,128)(2,1)}), bf16[16,384,160]{1,2,0:T(8,128)(2,1)}, u32[]{:S(2)}, u32[]{:S(2)}) %all-to-all-start) | async-done | bytes 1966112 | tf_op jit(solution)/shard_map/all_to_all | solution.py:46
  189.1 2.1 subtract_convert_fusion
  191.2 0.2 copy-done.9
  191.4 1.2 fusion.9
  192.6 0.1 copy-done.4
  192.7 0.9 copy-done.1
  193.6 3.3 convolution_bitcast_fusion
  197.0 5.5 copy.24
  202.6 86.4 %reduce-scatter.10.cloned.1.call-done = f32[160,384]{1,0:T(8,128)} async-done(((f32[2560,384]{1,0:T(8,128)}), f32[160,384]{1,0:T(8,128)}) %reduce-scatter.10.cloned.1.call-update) | async-done | bytes 245776 | tf_op jit(solution)/shard_map/reduce_scatter | solution.py:70
  289.0 0.1 dynamic_slice.20
  289.1 3.8 convert_element_type.37
  292.9 33.6 %all-gather.8.cloned.1.call-done = f32[1280,384]{1,0:T(8,128)} async-done(((f32[160,384]{1,0:T(8,128)}), f32[1280,384]{1,0:T(8,128)}) %all-gather.8.cloned.1.call-update) | async-done | bytes 1966096 | tf_op jit(solution)/shard_map/all_gather | solution.py:11
  326.5 7.2 %while.28 = (s32[]{:T(128)}, f32[160,384]{1,0:T(8,128)S(1)}, s32[]{:T(128)}, f32[8,160,384]{2,1,0:T(8,128)}, s32[]{:T(128)}, /*index=5*/s32[]{:T(128)}) while((s32[]{:T(128)}, f32[160,384]{1,0:T(8,128)S(1)}, s32[]{:T(128)}, f32[8,160,384]{2,1,0:T(8,128)}, s32[]{:T(128)}, /*index=5*/s32[]{:T(128)}) %tuple.86), condition=%wide.region_6.7_spmd.clone, body=%wide.region_5.6_spmd.clone.sunk | while | flops 184324 | bytes 737373 | solution.py:21
  326.5 1.0 add_select_fusion.4
  327.6 1.0 add_select_fusion.4
  328.6 1.0 add_select_fusion.4
  329.6 1.0 add_select_fusion.4
  330.7 1.0 add_select_fusion.4
  331.7 1.0 add_select_fusion.4
  332.8 1.0 add_select_fusion.4
  333.8 2.3 multiply_reduce_fusion
  336.2 33.5 %all-gather.10.cloned.1.call-done = f32[1280,384]{1,0:T(8,128)} async-done(((f32[160,384]{1,0:T(8,128)}), f32[1280,384]{1,0:T(8,128)}) %all-gather.10.cloned.1.call-update) | async-done | bytes 1966096 | tf_op jit(solution)/shard_map/all_gather | solution.py:11
  369.7 3.0 rev.3
  372.6 7.3 %while.29 = (s32[]{:T(128)}, f32[160,384]{1,0:T(8,128)S(1)}, s32[]{:T(128)}, f32[8,160,384]{2,1,0:T(8,128)}, s32[]{:T(128)}, /*index=5*/s32[]{:T(128)}) while((s32[]{:T(128)}, f32[160,384]{1,0:T(8,128)S(1)}, s32[]{:T(128)}, f32[8,160,384]{2,1,0:T(8,128)}, s32[]{:T(128)}, /*index=5*/s32[]{:T(128)}) %tuple.68), condition=%wide.region_8.9_spmd.clone, body=%wide.region_7.8_spmd.clone.sunk | while | flops 184324 | bytes 737373 | solution.py:21
  372.6 1.1 add_select_fusion.5
  373.7 1.0 add_select_fusion.5
  374.8 1.0 add_select_fusion.5
  375.8 1.0 add_select_fusion.5
  376.8 1.0 add_select_fusion.5
  377.9 1.0 add_select_fusion.5
  378.9 1.0 add_select_fusion.5
  379.9 0.7 multiply_convert_fusion
  380.7 0.0 reduce-scatter.8.cloned.1.call-start
  380.7 47.0 %all-gather.6.cloned.1.call-done = bf16[2560,384]{1,0:T(8,128)(2,1)} async-done(((bf16[160,384]{1,0:T(8,128)(2,1)}), bf16[2560,384]{1,0:T(8,128)(2,1)}) %all-gather.6.cloned.1.call-update) | async-done | bytes 1966096 | tf_op jit(solution)/shard_map/all_gather | solution.py:88
  427.7 5.9 %fusion.32 = f32[512,2560]{1,0:T(8,128)} fusion(bf16[2560,384]{1,0:T(8,128)(2,1)} %all-gather.6.cloned.1.call-done, f32[384,512]{1,0:T(8,128)} %copy-done.1, pred[512]{0:T(512)(128)(4,1)S(1)} %add_compare_fusion), kind=kOutput, calls=%fused_computation.44 | convolution fusion | flops 1008402432 | bytes 7995904 | tf_op jit(solution)/shard_map/dot_general | solution.py:93
  433.7 1.1 copy-done.2
  434.7 7.2 %fusion.11 = f32[2560,512]{1,0:T(8,128)} fusion(bf16[384,2560]{0,1:T(8,128)(2,1)} %copy-done.4, bf16[2560,384]{1,0:T(8,128)(2,1)} %all-gather.6.cloned.1.call-done, bf16[512,2560]{1,0:T(8,128)(2,1)S(1)} %copy-done, f32[384,512]{1,0:T(8,128)S(1)} %copy-done.2, pred[512]{0:T(512)(128)(4,1)S(1)} %add_compare_fusion), kind=kOutput, calls=%fused_computation.19 | convolution fusion | flops 2014445568 | bytes 12583424 | tf_op jit(solution)/shard_map/dot_general | solution.py:97
  442.0 70.6 %psum.31 = f32[]{:T(128)} all-reduce(f32[]{:T(128)} %get-tuple-element.215), channel_id=1, replica_groups=mesh['seg'=8,'shard'=16,'tok'=2] {'shard','tok'}, use_global_device_ids=true, to_apply=%region_12.13 | all-reduce | flops 1 | bytes 8 | tf_op jit(solution)/shard_map/psum | solution.py:84
  513.2 69.1 %reduce-scatter.6.cloned.1.call-done = f32[1280,512]{1,0:T(8,128)} async-done(((f32[2560,512]{1,0:T(8,128)}), f32[1280,512]{1,0:T(8,128)}) %reduce-scatter.6.cloned.1.call-update) | async-done | bytes 2621456 | tf_op jit(solution)/shard_map/reduce_scatter | solution.py:100
  (38 shorter events, 0.4 us)
Async XLA Ops:
  7.2 186.5 %copy-start = (bf16[512,2560]{1,0:T(8,128)(2,1)S(1)}, bf16[512,2560]{1,0:T(8,128)(2,1)}, u32[]{:S(2)}) copy-start(bf16[512,2560]{1,0:T(8,128)(2,1)} %param.19) | copy-start | bytes 7864324
  7.2 3.0 copy-start.6
  7.2 3.0 copy-start.7
  7.2 119.6 %all-reduce.4.cloned.1.call-start = ((), (), s32[]{:S(2)}) async-start(), calls=%async_computation.10 | async-start | bytes 7864320 | tf_op jit(solution)/shard_map/psum | solution.py:41
  11.9 114.8 %copy-start.10 = (bf16[1280,160]{0,1:T(8,128)(2,1)S(1)}, bf16[1280,160]{0,1:T(8,128)(2,1)}, u32[]{:S(2)}) copy-start(bf16[1280,160]{0,1:T(8,128)(2,1)} %param.16) | copy-start | bytes 1228804
  161.6 5.3 copy-start.12
  161.6 27.5 %copy-start.8 = (f32[2560]{0:T(1024)S(1)}, f32[2560]{0:T(1024)}, u32[]{:S(2)}) copy-start(f32[2560]{0:T(1024)} %param.20) | copy-start | bytes 30724
  161.6 27.5 %all-to-all-start = ((bf16[16,384,160]{1,2,0:T(8,128)(2,1)}), bf16[16,384,160]{1,2,0:T(8,128)(2,1)}, u32[]{:S(2)}, u32[]{:S(2)}) async-start(bf16[16,384,160]{1,2,0:T(8,128)(2,1)} %stack.2), calls=%async_computation | async-start | bytes 3932160 | tf_op jit(solution)/shard_map/all_to_all | solution.py:46
  166.9 122.1 %reduce-scatter.10.cloned.1.call-start = ((), (), s32[]{:S(2)}) async-start(), calls=%async_computation.9 | async-start | bytes 4177920 | tf_op jit(solution)/shard_map/reduce_scatter | solution.py:70
  168.2 23.0 %copy-start.11 = (f32[512]{0:T(512)S(1)}, f32[512]{0:T(512)}, u32[]{:S(2)}) copy-start(f32[512]{0:T(512)} %param.18) | copy-start | bytes 6148
  189.1 2.3 copy-start.9
  191.4 1.3 copy-start.4
  192.7 0.9 copy-start.1
  202.5 124.0 %all-gather.8.cloned.1.call-start = ((), (), s32[]{:S(2)}) async-start(), calls=%async_computation.7 | async-start | bytes 2211840 | tf_op jit(solution)/shard_map/all_gather | solution.py:11
  289.0 80.7 %all-gather.10.cloned.1.call-start = ((), (), s32[]{:S(2)}) async-start(), calls=%async_computation.8 | async-start | bytes 2211840 | tf_op jit(solution)/shard_map/all_gather | solution.py:11
  292.9 40.9 %copy-start.5 = (f32[160,384]{1,0:T(8,128)S(1)}, f32[160,384]{1,0:T(8,128)}, u32[]{:S(2)}) copy-start(f32[160,384]{1,0:T(8,128)} %reduce-scatter.10.cloned.1.call-done) | copy-start | bytes 737284
  336.2 91.5 %all-gather.6.cloned.1.call-start = ((), (), s32[]{:S(2)}) async-start(), calls=%async_computation.4 | async-start | bytes 2088960 | tf_op jit(solution)/shard_map/all_gather | solution.py:88
  372.6 7.3 %copy-start.3 = (f32[160,384]{1,0:T(8,128)S(1)}, f32[160,384]{1,0:T(8,128)}, u32[]{:S(2)}) copy-start(f32[160,384]{1,0:T(8,128)} %get-tuple-element.216) | copy-start | bytes 737284
  380.7 132.5 %reduce-scatter.8.cloned.1.call-start = ((), (), s32[]{:S(2)}) async-start(), calls=%async_computation.6 | async-start | bytes 7864320 | tf_op jit(solution)/shard_map/reduce_scatter | solution.py:101
  433.6 1.1 copy-start.2
  433.6 148.7 %reduce-scatter.6.cloned.1.call-start = ((), (), s32[]{:S(2)}) async-start(), calls=%async_computation.5 | async-start | bytes 7864320 | tf_op jit(solution)/shard_map/reduce_scatter | solution.py:100
Sparse Core Ops, SparseCore 0:
  12.1 114.6 all-reduce.3
  202.6 86.2 reduce-scatter.9
  290.8 35.7 all-gather.7
  336.3 33.3 all-gather.9
  380.8 46.8 all-gather.5
  433.8 73.9 reduce-scatter.7
  510.9 71.4 reduce-scatter.5
